TPU v7x, 512 devices: a whole 4x4x16 slice. The times are simulated.
512 devices in a mesh: ctx: 16 (over z), exp: 32 (over y, x, core).
Axes of the slice: x: 4, y: 4, z: 16, core: 2. Of those that a mesh axis runs over, the one named last changes fastest.
Arguments:
- tokens: bfloat16 [65536, 2048], P(('ctx', 'exp')), may hold values from -6 to 6
- expert_ids: int32 [65536, 1], P(('ctx', 'exp')), may hold values from 0 to 31; in each aligned block of 128 rows (0 to 127, 128 to 255, ...) at most 5 rows name the same one
- gate_weights: float32 [65536, 1], P(('ctx', 'exp')), may hold values from 0.1 to 1
- weight_gate: bfloat16 [32, 2048, 1024], P('exp', 'ctx'), may hold values from -0.125 to 0.125
- weight_up: bfloat16 [32, 2048, 1024], P('exp', 'ctx'), may hold values from -0.125 to 0.125
- weight_down: bfloat16 [32, 1024, 2048], P('exp', None, 'ctx'), may hold values from -0.1875 to 0.1875
- attn_queries: bfloat16 [65536, 2048], P(('ctx', 'exp')), may hold values from -6 to 6
- attn_keys: bfloat16 [65536, 2048], P(('ctx', 'exp')), may hold values from -6 to 6
- grad_out: bfloat16 [65536, 2048], P('ctx', 'exp'), may hold values from -6 to 6
Outputs:
- grad_tokens: bfloat16 [65536, 2048], P(('ctx', 'exp'))
- grad_queries: bfloat16 [65536, 2048], P(('ctx', 'exp'))
- grad_keys: bfloat16 [65536, 2048], P(('ctx', 'exp'))
Inputs may be any that keep to these rules, and one draw needn't show every extreme that they name: `expert_ids`: each row names one expert. Within each aligned block of 128 rows (the rows of one device), no expert is named more than 5 times, a bound that some block reaches.
All inputs are finite; a program needn't handle non-finite values.
Results may differ from a plain program's by a relative error of at most 0.0085.
Values may be sent and summed in bfloat16 or wider, within the bound.
A program may use at most 64 MiB of HBM per device.

v0:
```python
import math

import jax
import jax.numpy as jnp
from jax import lax
from jax.sharding import PartitionSpec as P

HEAD_DIM = 128
TOPK = 1
BLOCK = 512


def silu_parts(gate_pre):
    sigmoid = jax.nn.sigmoid(gate_pre)
    activation = gate_pre * sigmoid
    silu_slope = sigmoid * (1.0 + gate_pre * (1.0 - sigmoid))
    return (activation, silu_slope)


def expert_move(buffer):
    return lax.all_to_all(buffer, "exp", split_axis=0, concat_axis=0, tiled=True)


def contract_rows(left, right):
    return lax.dot_general(
        left, right, (((1,), (1,)), ((), ())), preferred_element_type=jnp.float32
    )


def block_grads(block_item, attn_scale):
    query_blk, key_blk, value_blk, cot_blk, state_start, state_after = block_item
    length = query_blk.shape[1]
    causal = (jnp.arange(length)[:, None] >= jnp.arange(length)[None, :])[None]
    scores = jnp.where(
        causal,
        jnp.einsum("htd,hsd->hts", query_blk, key_blk, preferred_element_type=jnp.float32),
        0.0,
    ).astype(jnp.bfloat16)
    probes = jnp.where(
        causal,
        jnp.einsum("htv,hsv->hts", cot_blk, value_blk, preferred_element_type=jnp.float32),
        0.0,
    ).astype(jnp.bfloat16)
    start_low = state_start.astype(jnp.bfloat16)
    after_low = state_after.astype(jnp.bfloat16)
    grad_query = attn_scale * (
        jnp.einsum("hts,hsd->htd", probes, key_blk, preferred_element_type=jnp.float32)
        + jnp.einsum("htv,hdv->htd", cot_blk, start_low, preferred_element_type=jnp.float32)
    )
    grad_key = attn_scale * (
        jnp.einsum("hts,htd->hsd", probes, query_blk, preferred_element_type=jnp.float32)
        + jnp.einsum("hsv,hdv->hsd", value_blk, after_low, preferred_element_type=jnp.float32)
    )
    grad_value = attn_scale * (
        jnp.einsum("hts,htv->hsv", scores, cot_blk, preferred_element_type=jnp.float32)
        + jnp.einsum("hsd,hdv->hsv", key_blk, after_low, preferred_element_type=jnp.float32)
    )
    return (
        grad_query.astype(jnp.bfloat16),
        grad_key.astype(jnp.bfloat16),
        grad_value.astype(jnp.bfloat16),
    )


def shards(
    tokens,
    expert_ids,
    gate_weights,
    weight_gate,
    weight_up,
    weight_down,
    attn_queries,
    attn_keys,
    grad_out,
):
    exp_count = lax.axis_size("exp")
    ctx_count = lax.axis_size("ctx")
    row_count, model_width = tokens.shape
    experts = weight_gate.shape[0] * exp_count
    capacity = 5 * row_count * TOPK // (4 * exp_count)
    flat_ids = expert_ids.reshape(-1)
    one_hot = (flat_ids[:, None] == jnp.arange(experts, dtype=jnp.int32)[None, :]).astype(jnp.int32)
    slot_rank = jnp.sum((jnp.cumsum(one_hot, axis=0, dtype=jnp.int32) - one_hot) * one_hot, axis=1)
    slot_dest = flat_ids * capacity + slot_rank
    slot_owner = jnp.arange(row_count * TOPK, dtype=jnp.int32) // TOPK
    slot_source = (
        jnp.full((experts * capacity,), row_count, jnp.int32).at[slot_dest].set(slot_owner)
    )
    dest_table = slot_dest.reshape(row_count, TOPK)
    padded = jnp.concatenate([tokens, jnp.zeros((1, model_width), jnp.bfloat16)], axis=0)
    slot_rows = expert_move(padded[slot_source].reshape(experts, capacity, model_width)).reshape(
        -1, model_width
    )
    full_gate, full_up, full_down = (
        lax.all_gather(weight_gate, "ctx", axis=1, tiled=True),
        lax.all_gather(weight_up, "ctx", axis=1, tiled=True),
        lax.all_gather(weight_down, "ctx", axis=2, tiled=True),
    )
    weight_one = full_gate[0]
    weight_three = full_up[0]
    weight_two = full_down[0]
    gate_pre = jnp.dot(slot_rows, weight_one, preferred_element_type=jnp.float32)
    up_proj = jnp.dot(slot_rows, weight_three, preferred_element_type=jnp.float32)
    activation, silu_slope = silu_parts(gate_pre)
    hidden = (activation * up_proj).astype(jnp.bfloat16)
    expert_out = jnp.dot(hidden, weight_two, preferred_element_type=jnp.float32).astype(
        jnp.bfloat16
    )
    returned = expert_move(expert_out.reshape(exp_count, capacity, model_width)).reshape(
        -1, model_width
    )
    choice_index = 0
    values_sum = gate_weights * returned[dest_table[:, choice_index]].astype(jnp.float32)
    values_mixed = values_sum.astype(jnp.bfloat16)
    part_width = model_width // exp_count
    key_width = max(part_width, HEAD_DIM)
    group_size = key_width // part_width
    local_heads = key_width // HEAD_DIM
    value_width = part_width // local_heads
    span_rows = row_count * exp_count
    attn_scale = 1.0 / math.sqrt(HEAD_DIM * span_rows * ctx_count)
    values_split = jnp.transpose(values_mixed.reshape(row_count, exp_count, part_width), (1, 0, 2))
    query_copies = jnp.repeat(
        jnp.transpose(
            attn_queries.reshape(row_count, model_width // key_width, key_width), (1, 0, 2)
        ),
        group_size,
        axis=0,
    )
    key_copies = jnp.repeat(
        jnp.transpose(attn_keys.reshape(row_count, model_width // key_width, key_width), (1, 0, 2)),
        group_size,
        axis=0,
    )
    value_in, query_in, key_in = (
        lax.all_to_all(values_split, "exp", split_axis=0, concat_axis=0, tiled=True),
        lax.all_to_all(query_copies, "exp", split_axis=0, concat_axis=0, tiled=True),
        lax.all_to_all(key_copies, "exp", split_axis=0, concat_axis=0, tiled=True),
    )
    query_full = query_in.reshape(span_rows, key_width)
    key_full = key_in.reshape(span_rows, key_width)
    nblocks = span_rows // BLOCK

    def to_blocks(flat, width):
        return jnp.transpose(flat.reshape(nblocks, BLOCK, local_heads, width), (0, 2, 1, 3))

    def from_blocks(blocked):
        return jnp.transpose(blocked, (0, 2, 1, 3)).reshape(span_rows, -1)

    query_blocks = to_blocks(query_full, HEAD_DIM)
    key_blocks = to_blocks(key_full, HEAD_DIM)
    value_blocks = to_blocks(value_in.reshape(span_rows, part_width), value_width)
    cot_blocks = to_blocks(grad_out, value_width)
    state_blocks = jnp.einsum(
        "nhbd,nhbv->nhdv", key_blocks, value_blocks, preferred_element_type=jnp.float32
    )
    after_blocks = jnp.einsum(
        "nhbd,nhbv->nhdv", query_blocks, cot_blocks, preferred_element_type=jnp.float32
    )
    state_local = jnp.sum(state_blocks, axis=0)
    after_local = jnp.sum(after_blocks, axis=0)
    every_state, every_after = (
        lax.all_gather(state_local[None], "ctx", axis=0, tiled=True),
        lax.all_gather(after_local[None], "ctx", axis=0, tiled=True),
    )
    position = lax.axis_index("ctx")
    order_ids = jnp.arange(ctx_count, dtype=jnp.int32)
    earlier = (order_ids < position).astype(jnp.float32).reshape(ctx_count, 1, 1, 1)
    later = (order_ids > position).astype(jnp.float32).reshape(ctx_count, 1, 1, 1)
    state_in = jnp.sum(every_state * earlier, axis=0)
    after_in = jnp.sum(every_after * later, axis=0)
    state_start = state_in[None] + jnp.cumsum(state_blocks, axis=0) - state_blocks
    state_after = after_in[None] + after_local[None] - jnp.cumsum(after_blocks, axis=0)

    def run_block(block_item):
        return block_grads(block_item, attn_scale)

    part_query, part_key, part_value = lax.map(
        run_block, (query_blocks, key_blocks, value_blocks, cot_blocks, state_start, state_after)
    )
    value_back = from_blocks(part_value).reshape(exp_count, row_count, part_width)
    flat_query = from_blocks(part_query)
    flat_key = from_blocks(part_key)
    grads_home, query_home, key_home = (
        lax.all_to_all(value_back, "exp", split_axis=0, concat_axis=0, tiled=True),
        lax.all_to_all(
            flat_query.reshape(exp_count, row_count, key_width),
            "exp",
            split_axis=0,
            concat_axis=0,
            tiled=True,
        ),
        lax.all_to_all(
            flat_key.reshape(exp_count, row_count, key_width),
            "exp",
            split_axis=0,
            concat_axis=0,
            tiled=True,
        ),
    )
    query_sum = jnp.sum(
        query_home.reshape(exp_count // group_size, group_size, row_count, key_width).astype(
            jnp.float32
        ),
        axis=1,
    ).astype(jnp.bfloat16)
    key_sum = jnp.sum(
        key_home.reshape(exp_count // group_size, group_size, row_count, key_width).astype(
            jnp.float32
        ),
        axis=1,
    ).astype(jnp.bfloat16)
    grad_queries = jnp.transpose(query_sum, (1, 0, 2)).reshape(row_count, model_width)
    grad_keys = jnp.transpose(key_sum, (1, 0, 2)).reshape(row_count, model_width)
    grads_mixed = jnp.transpose(grads_home, (1, 0, 2)).reshape(row_count, model_width)
    padded_grads = jnp.concatenate([grads_mixed, jnp.zeros((1, model_width), jnp.bfloat16)], axis=0)
    slot_grads = expert_move(
        padded_grads[slot_source].reshape(experts, capacity, model_width)
    ).reshape(-1, model_width)
    grad_hidden = contract_rows(slot_grads, weight_two)
    grad_gate = (grad_hidden * up_proj * silu_slope).astype(jnp.bfloat16)
    grad_up = (grad_hidden * activation).astype(jnp.bfloat16)
    expert_grad = (
        contract_rows(grad_gate, weight_one) + contract_rows(grad_up, weight_three)
    ).astype(jnp.bfloat16)
    grad_home = expert_move(expert_grad.reshape(exp_count, capacity, model_width)).reshape(
        -1, model_width
    )
    choice_index = 0
    grad_sum = gate_weights * grad_home[dest_table[:, choice_index]].astype(jnp.float32)
    grad_tokens = grad_sum.astype(jnp.bfloat16)
    return (grad_tokens, grad_queries, grad_keys)


def solution(mesh):
    in_specs = (
        P(("ctx", "exp"), None),
        P(("ctx", "exp"), None),
        P(("ctx", "exp"), None),
        P("exp", "ctx", None),
        P("exp", "ctx", None),
        P("exp", None, "ctx"),
        P(("ctx", "exp"), None),
        P(("ctx", "exp"), None),
        P("ctx", "exp"),
    )
    out_specs = (P(("ctx", "exp"), None), P(("ctx", "exp"), None), P(("ctx", "exp"), None))
    return jax.shard_map(shards, mesh=mesh, in_specs=in_specs, out_specs=out_specs, check_vma=False)
```

profile of v0, /device:TPU:1, one launch (start us, length us, event | category | flops | bytes accessed | tf_op | source)
XLA Modules:
  0.0 574.1 jit_solution(14551951014416149329)
XLA Ops:
  15.2 26.7 %all_to_all.50 = bf16[32,5,2048]{2,1,0:T(8,128)(2,1)S(1)} all-to-all(bf16[32,5,2048]{2,1,0:T(8,128)(2,1)S(1)} %reshape.210), channel_id=1, replica_groups=mesh['ctx'=16,'exp'=32] {'exp'}, dimensions={0} | all-to-all | bytes 1310720 | tf_op jit(solution)/shard_map/all_to_all | solution.py:21
  42.2 42.5 %all-gather.6.cloned.1.call-done = bf16[1,2048,1024]{2,1,0:T(8,128)(2,1)} async-done(((bf16[1,128,1024]{2,1,0:T(8,128)(2,1)}), bf16[1,2048,1024]{2,1,0:T(8,128)(2,1)}) %all-gather.6.cloned.1.call-update) | async-done | bytes 4194320 | tf_op jit(solution)/shard_map/all_gather | solution.py:95
  84.6 3.0 fusion.67
  87.7 73.5 %all-gather.8.cloned.1.call-done = bf16[1,2048,1024]{2,1,0:T(8,128)(2,1)} async-done(((bf16[1,128,1024]{2,1,0:T(8,128)(2,1)}), bf16[1,2048,1024]{2,1,0:T(8,128)(2,1)}) %all-gather.8.cloned.1.call-update) | async-done | bytes 4194320 | tf_op jit(solution)/shard_map/all_gather | solution.py:96
  161.1 3.0 fusion.63
  164.2 89.2 %all-gather.10.cloned.1.call-done = bf16[1,1024,2048]{2,1,0:T(8,128)(2,1)} async-done(((bf16[1,1024,128]{2,1,0:T(8,128)(2,1)}), bf16[1,1024,2048]{2,1,0:T(8,128)(2,1)}) %all-gather.10.cloned.1.call-update) | async-done | bytes 4194320 | tf_op jit(solution)/shard_map/all_gather | solution.py:97
  253.4 3.1 fusion.72
  256.5 1.3 reshape.212
  257.8 16.7 %all-to-all-start.1 = ((bf16[32,5,2048]{2,1,0:T(8,128)(2,1)}), bf16[32,5,2048]{2,1,0:T(8,128)(2,1)S(1)}, u32[]{:S(2)}, u32[]{:S(2)}) async-start(bf16[32,5,2048]{2,1,0:T(8,128)(2,1)} %reshape.212), calls=%async_computation.1 | async-start | bytes 2097152 | tf_op jit(solution)/shard_map/all_to_all | solution.py:21
  274.7 16.8 %all-to-all-done.1 = bf16[32,5,2048]{2,1,0:T(8,128)(2,1)S(1)} async-done(((bf16[32,5,2048]{2,1,0:T(8,128)(2,1)}), bf16[32,5,2048]{2,1,0:T(8,128)(2,1)S(1)}, u32[]{:S(2)}, u32[]{:S(2)}) %all-to-all-start.1) | async-done | bytes 655392 | tf_op jit(solution)/shard_map/all_to_all | solution.py:21
  292.7 4.0 all-to-all-start.4
  299.1 14.8 %all-to-all-done.4 = bf16[32,128,128]{2,1,0:T(8,128)(2,1)S(1)} async-done(((bf16[32,128,128]{2,1,0:T(8,128)(2,1)}), bf16[32,128,128]{2,1,0:T(8,128)(2,1)S(1)}, u32[]{:S(2)}, u32[]{:S(2)}) %all-to-all-start.4) | async-done | bytes 1048608 | tf_op jit(solution)/shard_map/all_to_all | solution.py:137
  313.9 3.9 all-to-all-start.2
  319.1 10.2 %all-to-all-done.2 = bf16[32,128,64]{1,2,0:T(8,128)(2,1)S(1)} async-done(((bf16[32,128,64]{1,2,0:T(8,128)(2,1)}), bf16[32,128,64]{1,2,0:T(8,128)(2,1)S(1)}, u32[]{:S(2)}, u32[]{:S(2)}) %all-to-all-start.2) | async-done | bytes 524320 | tf_op jit(solution)/shard_map/all_to_all | solution.py:136
  330.6 4.0 all-to-all-start.3
  334.6 1.4 copy.59
  336.3 25.6 %all-gather.1 = f32[2048,64]{0,1:T(8,128)S(1)} all-gather(f32[128,64]{0,1:T(8,128)S(1)} %get-tuple-element.137), channel_id=3, replica_groups=mesh['ctx'=16,'exp'=32] {'ctx'}, dimensions={0}, use_global_device_ids=true | all-gather | bytes 557056 | tf_op jit(solution)/shard_map/all_gather | solution.py:164
  363.4 1.4 reshape.216
  365.1 22.5 %all-gather = f32[2048,64]{0,1:T(8,128)S(1)} all-gather(f32[128,64]{0,1:T(8,128)S(1)} %get-tuple-element.135), channel_id=2, replica_groups=mesh['ctx'=16,'exp'=32] {'ctx'}, dimensions={0}, use_global_device_ids=true | all-gather | bytes 557056 | tf_op jit(solution)/shard_map/all_gather | solution.py:163
  388.0 1.3 copy.77
  389.3 58.1 %while.14 = (s32[]{:T(128)}, bf16[8,1,512,128]{3,2,1,0:T(8,128)(2,1)}, bf16[8,1,512,128]{3,2,1,0:T(8,128)(2,1)}, bf16[8,1,512,64]{2,3,1,0:T(8,128)(2,1)S(1)}, bf...) while((s32[]{:T(128)}, ...), condition=%wide.region_10.11_spmd, body=%wide.region_9.10_spmd.sunk | while | flops 295665664 | bytes 4724353 | solution.py:178
  389.6 1.4 fusion.151
  391.1 1.3 fusion.146
  393.1 1.8 fusion.148
  394.8 1.7 fusion.150
  396.8 1.4 fusion.151
  398.4 1.3 fusion.146
  400.3 1.8 fusion.148
  402.1 1.7 fusion.150
  404.1 1.4 fusion.151
  405.6 1.3 fusion.146
  407.6 1.8 fusion.148
  409.3 1.7 fusion.150
  411.3 1.4 fusion.151
  412.9 1.3 fusion.146
  414.8 1.7 fusion.148
  416.6 1.7 fusion.150
  418.6 1.4 fusion.151
  420.1 1.3 fusion.146
  422.1 1.8 fusion.148
  423.8 1.8 fusion.150
  425.8 1.4 fusion.151
  427.4 1.3 fusion.146
  429.3 1.8 fusion.148
  431.1 1.7 fusion.150
  433.1 1.4 fusion.151
  434.7 1.3 fusion.146
  436.6 1.8 fusion.148
  438.4 1.8 fusion.150
  440.4 1.4 fusion.151
  443.9 1.8 fusion.148
  445.7 1.7 fusion.150
  448.2 31.5 %all_to_all.51 = bf16[32,128,64]{1,2,0:T(8,128)(2,1)S(1)} all-to-all(bf16[32,128,64]{1,2,0:T(8,128)(2,1)S(1)} %copy.71), channel_id=1, replica_groups=mesh['ctx'=16,'exp'=32] {'exp'}, dimensions={0} | all-to-all | bytes 1048576 | tf_op jit(solution)/shard_map/all_to_all | solution.py:185
  481.3 20.7 %all_to_all.52 = bf16[32,5,2048]{2,1,0:T(8,128)(2,1)S(1)} all-to-all(bf16[32,5,2048]{2,1,0:T(8,128)(2,1)S(1)} %reshape.223), channel_id=1, replica_groups=mesh['ctx'=16,'exp'=32] {'exp'}, dimensions={0} | all-to-all | bytes 1310720 | tf_op jit(solution)/shard_map/all_to_all | solution.py:21
  502.0 4.0 all-to-all-start.8
  506.3 16.9 %all-to-all-done.8 = bf16[32,128,128]{2,1,0:T(8,128)(2,1)S(1)} async-done(((bf16[32,128,128]{2,1,0:T(8,128)(2,1)}), bf16[32,128,128]{2,1,0:T(8,128)(2,1)S(1)}, u32[]{:S(2)}, u32[]{:S(2)}) %all-to-all-start.8) | async-done | bytes 1048608 | tf_op jit(solution)/shard_map/all_to_all | solution.py:186
  523.1 4.0 all-to-all-start.9
  527.1 3.9 fusion.57
  531.0 1.5 fusion.61
  533.4 1.6 fusion.75
  536.2 8.1 %all-to-all-done.9 = bf16[32,128,128]{2,1,0:T(8,128)(2,1)S(1)} async-done(((bf16[32,128,128]{2,1,0:T(8,128)(2,1)}), bf16[32,128,128]{2,1,0:T(8,128)(2,1)S(1)}, u32[]{:S(2)}, u32[]{:S(2)}) %all-to-all-start.9) | async-done | bytes 1048608 | tf_op jit(solution)/shard_map/all_to_all | solution.py:193
  544.3 4.0 all-to-all-start.7
  549.3 1.3 copy.73
  553.1 12.4 %all-to-all-done.7 = bf16[32,5,2048]{2,1,0:T(8,128)(2,1)S(1)} async-done(((bf16[32,5,2048]{2,1,0:T(8,128)(2,1)}), bf16[32,5,2048]{2,1,0:T(8,128)(2,1)S(1)}, u32[]{:S(2)}, u32[]{:S(2)}) %all-to-all-start.7) | async-done | bytes 655392 | tf_op jit(solution)/shard_map/all_to_all | solution.py:21
  (131 shorter events, 37.4 us)
Async XLA Ops:
  7.2 77.4 %all-gather.6.cloned.1.call-start = ((), (), s32[]{:S(2)}) async-start(), calls=%async_computation.10 | async-start | bytes 4456448 | tf_op jit(solution)/shard_map/all_gather | solution.py:95
  7.9 153.2 %all-gather.8.cloned.1.call-start = ((), (), s32[]{:S(2)}) async-start(), calls=%async_computation.11 | async-start | bytes 4456448 | tf_op jit(solution)/shard_map/all_gather | solution.py:96
  8.6 244.8 %all-gather.10.cloned.1.call-start = ((), (), s32[]{:S(2)}) async-start(), calls=%async_computation.12 | async-start | bytes 4456448 | tf_op jit(solution)/shard_map/all_gather | solution.py:97
  87.6 168.8 %copy-start.3 = (f32[160,1024]{1,0:T(8,128)}, f32[160,1024]{1,0:T(8,128)S(1)}, u32[]{:S(2)}) copy-start(f32[160,1024]{1,0:T(8,128)S(1)} %fusion.67) | copy-start | bytes 1966084
  164.2 93.6 %copy-start.5 = (f32[160,1024]{1,0:T(8,128)}, f32[160,1024]{1,0:T(8,128)S(1)}, u32[]{:S(2)}) copy-start(f32[160,1024]{1,0:T(8,128)S(1)} %fusion.63) | copy-start | bytes 1966084
  164.2 110.2 %copy-start.7 = (bf16[128,2048]{1,0:T(8,128)(2,1)S(1)}, bf16[128,2048]{1,0:T(8,128)(2,1)}, u32[]{:S(2)}) copy-start(bf16[128,2048]{1,0:T(8,128)(2,1)} %param.17) | copy-start | bytes 1572868
  257.8 33.7 %all-to-all-start.1 = ((bf16[32,5,2048]{2,1,0:T(8,128)(2,1)}), bf16[32,5,2048]{2,1,0:T(8,128)(2,1)S(1)}, u32[]{:S(2)}, u32[]{:S(2)}) async-start(bf16[32,5,2048]{2,1,0:T(8,128)(2,1)} %reshape.212), calls=%async_computation.1 | async-start | bytes 2097152 | tf_op jit(solution)/shard_map/all_to_all | solution.py:21
  292.7 21.1 %all-to-all-start.4 = ((bf16[32,128,128]{2,1,0:T(8,128)(2,1)}), bf16[32,128,128]{2,1,0:T(8,128)(2,1)S(1)}, u32[]{:S(2)}, u32[]{:S(2)}) async-start(bf16[32,128,128]{2,1,0:T(8,128)(2,1)} %bitcast.27), calls=%async_computation.4 | async-start | bytes 2097152 | tf_op jit(solution)/shard_map/all_to_all | solution.py:137
  296.7 1.5 copy-start.9
  298.2 36.4 %copy-start.2 = (bf16[4096,64]{0,1:T(8,128)(2,1)S(1)}, bf16[4096,64]{0,1:T(8,128)(2,1)}, u32[]{:S(2)}) copy-start(bf16[4096,64]{0,1:T(8,128)(2,1)} %param.19) | copy-start | bytes 1572868
  313.9 15.5 %all-to-all-start.2 = ((bf16[32,128,64]{1,2,0:T(8,128)(2,1)}), bf16[32,128,64]{1,2,0:T(8,128)(2,1)S(1)}, u32[]{:S(2)}, u32[]{:S(2)}) async-start(bf16[32,128,64]{1,2,0:T(8,128)(2,1)} %fusion.81), calls=%async_computation.2 | async-start | bytes 1048576 | tf_op jit(solution)/shard_map/all_to_all | solution.py:136
  330.6 34.1 %all-to-all-start.3 = ((bf16[32,128,128]{2,1,0:T(8,128)(2,1)}), bf16[32,128,128]{2,1,0:T(8,128)(2,1)S(1)}, u32[]{:S(2)}, u32[]{:S(2)}) async-start(bf16[32,128,128]{2,1,0:T(8,128)(2,1)} %bitcast.191), calls=%async_computation.3 | async-start | bytes 2097152 | tf_op jit(solution)/shard_map/all_to_all | solution.py:138
  365.1 24.2 %copy-start.8 = (bf16[8,1,512,64]{2,3,1,0:T(8,128)(2,1)S(1)}, bf16[8,1,512,64]{2,3,1,0:T(8,128)(2,1)}, u32[]{:S(2)}) copy-start(bf16[8,1,512,64]{2,3,1,0:T(8,128)(2,1)} %custom-call.10) | copy-start | bytes 1572868
  502.0 21.1 %all-to-all-start.8 = ((bf16[32,128,128]{2,1,0:T(8,128)(2,1)}), bf16[32,128,128]{2,1,0:T(8,128)(2,1)S(1)}, u32[]{:S(2)}, u32[]{:S(2)}) async-start(bf16[32,128,128]{2,1,0:T(8,128)(2,1)} %bitcast.33), calls=%async_computation.8 | async-start | bytes 2097152 | tf_op jit(solution)/shard_map/all_to_all | solution.py:186
  506.2 24.7 %copy-start.4 = (f32[160,1024]{1,0:T(8,128)S(1)}, f32[160,1024]{1,0:T(8,128)}, u32[]{:S(2)}) copy-start(f32[160,1024]{1,0:T(8,128)} %copy-done.3) | copy-start | bytes 1966084
  523.1 21.1 %all-to-all-start.9 = ((bf16[32,128,128]{2,1,0:T(8,128)(2,1)}), bf16[32,128,128]{2,1,0:T(8,128)(2,1)S(1)}, u32[]{:S(2)}, u32[]{:S(2)}) async-start(bf16[32,128,128]{2,1,0:T(8,128)(2,1)} %bitcast.205), calls=%async_computation.9 | async-start | bytes 2097152 | tf_op jit(solution)/shard_map/all_to_all | solution.py:193
  527.1 3.9 copy-start.1
  531.0 2.2 copy-start
  531.0 2.3 copy-start.6
  544.3 21.1 %all-to-all-start.7 = ((bf16[32,5,2048]{2,1,0:T(8,128)(2,1)}), bf16[32,5,2048]{2,1,0:T(8,128)(2,1)S(1)}, u32[]{:S(2)}, u32[]{:S(2)}) async-start(bf16[32,5,2048]{2,1,0:T(8,128)(2,1)} %reshape.225), calls=%async_computation.7 | async-start | bytes 2097152 | tf_op jit(solution)/shard_map/all_to_all | solution.py:21
Sparse Core Ops, SparseCore 0:
  10.0 74.5 all-gather.5
  86.7 74.4 all-gather.7
  163.2 90.2 all-gather.9
where the time goes:
time: 576 us; the launch traced here: 574 us
  waiting for transfers between devices  286 us (50%)
  blocking collectives  127 us (22%)
  matrix products  72.7 us (13%)
  starting transfers between devices  40.6 us (7%)
  local copies, waits for them, and re-layouts  27.2 us (5%)
  between operations  14.3 us (2%)
  other arithmetic  5.9 us (1%)
    all_gather x1, waiting for transfers between devices, shards(): lax.all_gather(weight_down, 'ctx', axis=2, tiled=True)  89.2 us
    all_gather x1, waiting for transfers between devices, shards(): lax.all_gather(weight_up, 'ctx', axis=1, tiled=True)  73.5 us
    all_to_all x2, blocking collectives, expert_move(): lax.all_to_all(buffer, 'exp', split_axis=0, concat_axis=0, tiled=True)  47.3 us
    all_gather x1, waiting for transfers between devices, shards(): lax.all_gather(weight_gate, 'ctx', axis=1, tiled=True)  42.5 us
    all_to_all x1, blocking collectives, shards(): lax.all_to_all(value_back, 'exp', split_axis=0, concat_axis=0, tiled=True)  31.5 us
    all_to_all x2, waiting for transfers between devices, expert_move(): lax.all_to_all(buffer, 'exp', split_axis=0, concat_axis=0, tiled=True)  29.1 us
    all_gather x1, blocking collectives, shards(): lax.all_gather(after_local[None], 'ctx', axis=0, tiled=True)  25.6 us
    all_gather x1, blocking collectives, shards(): lax.all_gather(state_local[None], 'ctx', axis=0, tiled=True)  22.5 us
  transfers between devices with their start and end apart: 10, of which 9 were waited for; matrix products, arithmetic and copies ran while one was open for 6% of the time, Pallas kernels for 0%

commit v1 on v0

v1 whole, which is shorter than its diff:
```python
import math

import jax
import jax.numpy as jnp
from jax import lax
from jax.sharding import PartitionSpec as P

HEAD_DIM = 128
BLOCK = 512
CAP = 5


def exp_move(buffer):
    return lax.all_to_all(buffer, "exp", split_axis=0, concat_axis=0, tiled=True)


def dot32(spec, left, right):
    return jnp.einsum(spec, left, right, preferred_element_type=jnp.float32)


def split3(value):
    high = lax.reduce_precision(value, 8, 7)
    rest = value - high
    middle = lax.reduce_precision(rest, 8, 7)
    low = rest - middle
    return [part.astype(jnp.bfloat16) for part in (high, middle, low)]


def shards(tokens, expert_ids, gate_weights, weight_gate, weight_up, weight_down, attn_queries, attn_keys, grad_out):
    n_exp = lax.axis_size("exp")
    n_ctx = lax.axis_size("ctx")
    rows, width = tokens.shape
    slots = n_exp * CAP
    span = rows * n_exp
    part = width // n_exp
    heads = width // HEAD_DIM
    attn_scale = 1.0 / math.sqrt(HEAD_DIM * span * n_ctx)

    full_gate = lax.all_gather(weight_gate, "ctx", axis=1, tiled=True)[0]
    full_up = lax.all_gather(weight_up, "ctx", axis=1, tiled=True)[0]
    full_down = lax.all_gather(weight_down, "ctx", axis=2, tiled=True)[0]

    ids = expert_ids[:, 0]
    chosen = ids[:, None] == jnp.arange(n_exp, dtype=jnp.int32)[None, :]
    earlier_rows = jnp.arange(rows)[:, None] > jnp.arange(rows)[None, :]
    before = dot32("ij,je->ie", earlier_rows.astype(jnp.bfloat16), chosen.astype(jnp.bfloat16))
    rank = jnp.sum(jnp.where(chosen, before, 0.0), axis=1).astype(jnp.int32)
    dest = ids * CAP + rank
    place = (jnp.arange(slots, dtype=jnp.int32)[:, None] == dest[None, :]).astype(jnp.bfloat16)

    gate_parts = jnp.concatenate(split3(gate_weights) + [jnp.zeros((rows, HEAD_DIM - 3), jnp.bfloat16)], axis=1)
    packed = jnp.concatenate([tokens, gate_parts], axis=1)
    slot_rows = dot32("st,td->sd", place, packed).astype(jnp.bfloat16)
    arrived = exp_move(slot_rows.reshape(n_exp, CAP, width + HEAD_DIM)).reshape(slots, width + HEAD_DIM)
    expert_rows = arrived[:, :width]
    slot_gate = jnp.sum(arrived[:, width : width + 3].astype(jnp.float32), axis=1, keepdims=True)

    qkm = jnp.stack(
        [attn_queries.reshape(rows, heads, HEAD_DIM), attn_keys.reshape(rows, heads, HEAD_DIM)], axis=2
    )
    marks = jnp.broadcast_to(dest.astype(jnp.bfloat16)[:, None, None, None], (rows, heads, 1, HEAD_DIM))
    qkm = jnp.concatenate([qkm, marks], axis=2).reshape(rows, heads, 3 * HEAD_DIM)
    qkm = jnp.repeat(jnp.transpose(qkm, (1, 0, 2)), n_exp // heads, axis=0)
    qkm = exp_move(qkm)
    query = qkm[:, :, :HEAD_DIM].reshape(span, HEAD_DIM)
    key = qkm[:, :, HEAD_DIM : 2 * HEAD_DIM].reshape(span, HEAD_DIM)
    dest_all = qkm[:, :, 2 * HEAD_DIM].astype(jnp.int32)
    place_all = (jnp.arange(slots, dtype=jnp.int32)[None, :, None] == dest_all[:, None, :]).astype(jnp.bfloat16)

    nblocks = span // BLOCK
    qb = query.reshape(nblocks, BLOCK, HEAD_DIM)
    kb = key.reshape(nblocks, BLOCK, HEAD_DIM)
    gb = grad_out.reshape(nblocks, BLOCK, part)
    causal = (jnp.arange(BLOCK)[:, None] >= jnp.arange(BLOCK)[None, :])[None]
    position = lax.axis_index("ctx")
    levels = jnp.arange(n_ctx, dtype=jnp.int32)

    after_blocks = dot32("nbd,nbv->ndv", qb, gb)
    after_local = jnp.sum(after_blocks, axis=0)
    every_after = lax.all_gather(after_local, "ctx")
    after_in = jnp.sum(jnp.where((levels > position)[:, None, None], every_after, 0.0), axis=0)
    after = (after_in[None] + after_local[None] - jnp.cumsum(after_blocks, axis=0)).astype(jnp.bfloat16)
    scores = jnp.where(causal, dot32("ntd,nsd->nts", qb, kb), 0.0).astype(jnp.bfloat16)
    grad_value = (attn_scale * (dot32("nts,ntv->nsv", scores, gb) + dot32("nsd,ndv->nsv", kb, after))).astype(jnp.bfloat16)
    sent = dot32("dsm,dmv->dsv", place_all, grad_value.reshape(n_exp, rows, part)).astype(jnp.bfloat16)
    sent = jnp.transpose(sent.reshape(n_exp, n_exp, CAP, part), (1, 0, 2, 3))
    slot_grads = exp_move(sent.reshape(n_exp, slots, part))
    slot_grads = jnp.transpose(slot_grads, (1, 0, 2)).reshape(slots, width)

    gate_pre = dot32("rd,dh->rh", expert_rows, full_gate)
    up_proj = dot32("rd,dh->rh", expert_rows, full_up)
    sigmoid = jax.nn.sigmoid(gate_pre)
    activation = gate_pre * sigmoid
    slope = sigmoid * (1.0 + gate_pre * (1.0 - sigmoid))
    hidden = (activation * up_proj).astype(jnp.bfloat16)
    expert_out = lax.reduce_precision(dot32("rh,hd->rd", hidden, full_down), 8, 7)
    value_rows = (slot_gate * expert_out).astype(jnp.bfloat16)
    value_rows = jnp.transpose(value_rows.reshape(slots, n_exp, part), (1, 0, 2))
    value_rows = exp_move(value_rows).reshape(n_exp, n_exp, CAP, part)
    value_rows = jnp.transpose(value_rows, (1, 0, 2, 3)).reshape(n_exp, slots, part)
    value = dot32("dsm,dsv->dmv", place_all, value_rows).astype(jnp.bfloat16).reshape(span, part)
    vb = value.reshape(nblocks, BLOCK, part)

    state_blocks = dot32("nbd,nbv->ndv", kb, vb)
    state_local = jnp.sum(state_blocks, axis=0)
    every_state = lax.all_gather(state_local, "ctx")
    state_in = jnp.sum(jnp.where((levels < position)[:, None, None], every_state, 0.0), axis=0)
    start = (state_in[None] + jnp.cumsum(state_blocks, axis=0) - state_blocks).astype(jnp.bfloat16)
    probes = jnp.where(causal, dot32("ntv,nsv->nts", gb, vb), 0.0).astype(jnp.bfloat16)
    grad_query = attn_scale * (dot32("nts,nsd->ntd", probes, kb) + dot32("ntv,ndv->ntd", gb, start))
    grad_key = attn_scale * (dot32("nts,ntd->nsd", probes, qb) + dot32("nsv,ndv->nsd", vb, after))
    both = jnp.concatenate([grad_query.astype(jnp.bfloat16), grad_key.astype(jnp.bfloat16)], axis=2)
    home = exp_move(both.reshape(n_exp, rows, 2 * HEAD_DIM)).astype(jnp.float32)
    home = jnp.sum(home.reshape(heads, n_exp // heads, rows, 2 * HEAD_DIM), axis=1).astype(jnp.bfloat16)
    home = jnp.transpose(home, (1, 0, 2))
    grad_queries = home[:, :, :HEAD_DIM].reshape(rows, width)
    grad_keys = home[:, :, HEAD_DIM:].reshape(rows, width)

    grad_hidden = dot32("rd,hd->rh", slot_grads, full_down)
    grad_gate = (grad_hidden * up_proj * slope).astype(jnp.bfloat16)
    grad_up = (grad_hidden * activation).astype(jnp.bfloat16)
    expert_grad = dot32("rh,dh->rd", grad_gate, full_gate) + dot32("rh,dh->rd", grad_up, full_up)
    expert_grad = lax.reduce_precision(expert_grad, 8, 7)
    grad_rows = (slot_gate * expert_grad).astype(jnp.bfloat16)
    grad_home = exp_move(grad_rows.reshape(n_exp, CAP, width)).reshape(slots, width)
    grad_tokens = dot32("st,sd->td", place, grad_home).astype(jnp.bfloat16)
    return grad_tokens, grad_queries, grad_keys


def solution(mesh):
    rows = P(("ctx", "exp"), None)
    in_specs = (rows, rows, rows, P("exp", "ctx", None), P("exp", "ctx", None), P("exp", None, "ctx"), rows, rows, P("ctx", "exp"))
    return jax.shard_map(shards, mesh=mesh, in_specs=in_specs, out_specs=(rows, rows, rows), check_vma=False)
```

time: 576 us -> 394 us (0.68)
  waiting for transfers between devices: 286 us -> 173 us
  blocking collectives: 127 us -> 58.1 us
  matrix products: 72.7 us -> 38.2 us
  starting transfers between devices: 40.6 us -> 63.2 us
  local copies, waits for them, and re-layouts: 27.2 us -> 41.7 us
    all_gather x3, waiting for transfers between devices: 205 us -> 86 us  [the longest x1 86 us: shards(): full_down = lax.all_gather(weight_down, 'ctx', axis=2, tiled=True)[0]]
    all_to_all x3 -> x0, blocking collectives: 78.8 us -> none  [the longest x2 47.3 us: expert_move(): lax.all_to_all(buffer, 'exp', split_axis=0, concat_axis=0, tiled=True)]
    dot_general x64 -> x20, matrix products: 72.7 us -> 38.2 us  [dot32(): return jnp.einsum(spec, left, right, preferred_element_type=jnp.float32)]
    all_to_all x7 -> x6, starting transfers between devices: 40.5 us -> 63 us  [exp_move(): lax.all_to_all(buffer, 'exp', split_axis=0, concat_axis=0, tiled=True)]
    all_gather x2, blocking collectives: 48.1 us -> 58.1 us  [the longest x1 33.6 us: shards(): every_after = lax.all_gather(after_local, 'ctx')]
    reshape x9 -> x7, local copies, waits for them, and re-layouts: 4.33 us -> 11.7 us  [the longest x1 2.96 us: shards(): slot_grads = exp_move(sent.reshape(n_exp, slots, part))]
    slice x0 -> x7, local copies, waits for them, and re-layouts: none -> 6.75 us  [the longest x2 4.4 us: shards(): key = qkm[:, :, HEAD_DIM:2 * HEAD_DIM].reshape(span, HEAD_DIM)]
    all_to_all x7 -> x6, waiting for transfers between devices: 79.1 us -> 85.3 us  [exp_move(): lax.all_to_all(buffer, 'exp', split_axis=0, concat_axis=0, tiled=True)]
  transfers between devices with their start and end apart: 10 -> 9, of which waited for: 9 -> 5; matrix products, arithmetic and copies ran while one was open for 6% -> 20% of each run, Pallas kernels for 0% -> 0%
where the time goes in v1:
time: 394 us; the launch traced here: 393 us
  waiting for transfers between devices  173 us (44%)
  starting transfers between devices  63.2 us (16%)
  blocking collectives  58.1 us (15%)
  local copies, waits for them, and re-layouts  41.7 us (11%)
  matrix products  38.2 us (10%)
  between operations  14.3 us (4%)
  other arithmetic  4.24 us (1%)
    all_gather x1, waiting for transfers between devices, shards(): full_down = lax.all_gather(weight_down, 'ctx', axis=2, tiled=True)[0]  86 us
    all_to_all x6, waiting for transfers between devices, exp_move(): lax.all_to_all(buffer, 'exp', split_axis=0, concat_axis=0, tiled=True)  85.3 us
    all_to_all x6, starting transfers between devices, exp_move(): lax.all_to_all(buffer, 'exp', split_axis=0, concat_axis=0, tiled=True)  63 us
    dot_general x20, matrix products, dot32(): return jnp.einsum(spec, left, right, preferred_element_type=jnp.float32)  38.2 us
    all_gather x1, blocking collectives, shards(): every_after = lax.all_gather(after_local, 'ctx')  33.6 us
    all_gather x1, blocking collectives, shards(): every_state = lax.all_gather(state_local, 'ctx')  24.5 us
  transfers between devices with their start and end apart: 9, of which 5 were waited for; matrix products, arithmetic and copies ran while one was open for 20% of the time, Pallas kernels for 0%

profile of v1, /device:TPU:1, one launch (start us, length us, event | category | flops | bytes accessed | tf_op | source)
XLA Modules:
  0.0 393.1 jit_solution(8772777521789563003)
XLA Ops:
  7.2 0.7 all-gather.10.cloned.1.call-update
  8.0 0.7 all-gather.8.cloned.1.call-update
  8.7 0.7 all-gather.6.cloned.1.call-update
  9.4 0.7 fusion.82
  10.5 1.2 concatenate.9
  11.9 0.3 convolution_convert_fusion
  12.2 1.3 reshape.119
  13.5 10.6 %all-to-all-start = ((bf16[32,5,2176]{2,1,0:T(8,128)(2,1)}), bf16[32,5,2176]{2,1,0:T(8,128)(2,1)S(1)}, u32[]{:S(2)}, u32[]{:S(2)}) async-start(bf16[32,5,2176]{2,1,0:T(8,128)(2,1)} %reshape.119), calls=%async_computation | async-start | bytes 2228224 | tf_op jit(solution)/shard_map/all_to_all | solution.py:14
  24.4 1.0 copy.85
  25.5 1.2 pad_maximum_fusion.1
  26.7 15.2 %all-to-all-done = bf16[32,5,2176]{2,1,0:T(8,128)(2,1)S(1)} async-done(((bf16[32,5,2176]{2,1,0:T(8,128)(2,1)}), bf16[32,5,2176]{2,1,0:T(8,128)(2,1)S(1)}, u32[]{:S(2)}, u32[]{:S(2)}) %all-to-all-start) | async-done | bytes 696352 | tf_op jit(solution)/shard_map/all_to_all | solution.py:14
  42.0 2.6 broadcast_in_dim.71
  44.5 4.9 %all-to-all-start.1 = ((bf16[32,128,384]{1,2,0:T(8,128)(2,1)}), bf16[32,128,384]{1,2,0:T(8,128)(2,1)}, u32[]{:S(2)}, u32[]{:S(2)}) async-start(bf16[32,128,384]{1,2,0:T(8,128)(2,1)} %bitcast.5), calls=%async_computation.1 | async-start | bytes 6291456 | tf_op jit(solution)/shard_map/all_to_all | solution.py:14
  49.5 0.6 iota_compare_fusion.15
  50.1 0.8 iota_compare_fusion.7
  51.3 38.1 %all-to-all-done.1 = bf16[32,128,384]{1,2,0:T(8,128)(2,1)} async-done(((bf16[32,128,384]{1,2,0:T(8,128)(2,1)}), bf16[32,128,384]{1,2,0:T(8,128)(2,1)}, u32[]{:S(2)}, u32[]{:S(2)}) %all-to-all-start.1) | async-done | bytes 3145760 | tf_op jit(solution)/shard_map/all_to_all | solution.py:14
  89.4 2.8 fusion.88
  92.2 0.7 copy.88
  92.9 1.6 copy.89
  94.5 0.3 fusion.90
  94.8 33.6 %all-gather = f32[2048,64]{0,1:T(8,128)S(1)} all-gather(f32[128,64]{0,1:T(8,128)S(1)} %get-tuple-element.15), channel_id=2, replica_groups=mesh['ctx'=16,'exp'=32] {'ctx'}, dimensions={0}, use_global_device_ids=true | all-gather | bytes 557056 | tf_op jit(solution)/shard_map/all_gather | solution.py:80
  128.8 4.0 %fusion.1 = f32[8,512,64]{1,2,0:T(8,128)} fusion(pred[512,512]{1,0:T(8,128)(4,1)} %iota_compare_fusion.7, bf16[8,512,128]{2,1,0:T(8,128)(2,1)S(1)} %bitcast.125, bf16[8,512,128]{2,1,0:T(8,128)(2,1)S(1)} %bitcast.120, bf16[8,8,8,512]{3,2,1,0:T(8,128)(2,1)S(1)} %bitcast.141), kind=kOutput, calls=%fused_computation.3 | convolution fusion | flops 809500672 | bytes 3932160 | tf_op jit(solution)/shard_map/nts,ntv->nsv/dot_general | solution.py:18
  132.8 1.7 fusion.48
  134.8 1.1 reshape.124
  135.9 0.9 slice.29
  136.8 3.0 fusion.43
  139.8 3.0 copy.94
  142.8 2.9 copy.95
  145.7 3.0 copy.96
  148.6 11.8 %all-to-all-start.2 = ((bf16[32,160,64]{1,2,0:T(8,128)(2,1)}), bf16[32,160,64]{1,2,0:T(8,128)(2,1)}, u32[]{:S(2)}, u32[]{:S(2)}) async-start(bf16[32,160,64]{1,2,0:T(8,128)(2,1)} %copy.96), calls=%async_computation.2 | async-start | bytes 2097152 | tf_op jit(solution)/shard_map/all_to_all | solution.py:14
  160.5 3.9 fusion.4
  164.4 3.9 fusion.8
  168.3 86.0 %all-gather.6.cloned.1.call-done = bf16[1,1024,2048]{2,1,0:T(8,128)(2,1)} async-done(((bf16[1,1024,128]{2,1,0:T(8,128)(2,1)}), bf16[1,1024,2048]{2,1,0:T(8,128)(2,1)}) %all-gather.6.cloned.1.call-update) | async-done | bytes 4194320 | tf_op jit(solution)/shard_map/all_gather | solution.py:41
  254.2 4.4 %fusion.38 = bf16[160,2048]{1,0:T(8,128)(2,1)} fusion(bf16[1,1024,2048]{2,1,0:T(8,128)(2,1)} %all-gather.6.cloned.1.call-done, f32[160]{0:T(256)S(1)} %convert_reduce_fusion, f32[160,1024]{1,0:T(8,128)} %fusion.8, f32[160,1024]{1,0:T(8,128)} %fusion.4), kind=kOutput, calls=%fused_computation.29 | convolution fusion | flops 673054720 | bytes 6161024 | tf_op jit(solution)/shard_map/rh,hd->rd/dot_general | solution.py:18
  258.6 2.3 reshape.130
  260.9 2.0 copy.98
  262.9 16.7 %all-to-all-start.4 = ((bf16[32,160,64]{1,2,0:T(8,128)(2,1)}), bf16[32,160,64]{1,2,0:T(8,128)(2,1)S(1)}, u32[]{:S(2)}, u32[]{:S(2)}) async-start(bf16[32,160,64]{1,2,0:T(8,128)(2,1)} %copy.98), calls=%async_computation.4 | async-start | bytes 2097152 | tf_op jit(solution)/shard_map/all_to_all | solution.py:14
  279.6 4.2 %fusion.12 = f32[160,1024]{1,0:T(8,128)S(1)} fusion(bf16[160,2048]{0,1:T(8,128)(2,1)} %bitcast.13, bf16[1,1024,2048]{2,1,0:T(8,128)(2,1)} %all-gather.6.cloned.1.call-done), kind=kOutput, calls=%fused_computation.14 | convolution fusion | flops 671088640 | bytes 5505024 | tf_op jit(solution)/shard_map/rd,hd->rh/dot_general | solution.py:18
  283.9 1.6 fusion.2
  285.4 0.6 copy-done.3
  286.0 2.4 fusion.35
  288.4 2.2 reshape.128
  290.6 6.0 %all-to-all-done.4 = bf16[32,160,64]{1,2,0:T(8,128)(2,1)S(1)} async-done(((bf16[32,160,64]{1,2,0:T(8,128)(2,1)}), bf16[32,160,64]{1,2,0:T(8,128)(2,1)S(1)}, u32[]{:S(2)}, u32[]{:S(2)}) %all-to-all-start.4) | async-done | bytes 655392 | tf_op jit(solution)/shard_map/all_to_all | solution.py:14
  296.6 1.0 copy-done.4
  297.6 4.7 %all-to-all-start.3 = ((bf16[32,5,2048]{2,1,0:T(8,128)(2,1)}), bf16[32,5,2048]{2,1,0:T(8,128)(2,1)}, u32[]{:S(2)}, u32[]{:S(2)}) async-start(bf16[32,5,2048]{2,1,0:T(8,128)(2,1)} %reshape.128), calls=%async_computation.3 | async-start | bytes 2097152 | tf_op jit(solution)/shard_map/all_to_all | solution.py:14
  302.3 2.2 copy.99
  304.5 0.5 copy.100
  305.0 0.9 fusion.49
  305.9 0.3 copy.102
  306.6 2.5 fusion
  309.1 0.9 fusion.93
  310.0 1.5 fusion.92
  311.5 0.4 fusion.91
  311.9 0.6 multiply_convert_fusion
  312.5 24.5 %all-gather.1 = f32[2048,64]{0,1:T(8,128)S(1)} all-gather(f32[128,64]{0,1:T(8,128)S(1)} %get-tuple-element.17), channel_id=3, replica_groups=mesh['ctx'=16,'exp'=32] {'ctx'}, dimensions={0}, use_global_device_ids=true | all-gather | bytes 557056 | tf_op jit(solution)/shard_map/all_gather | solution.py:106
  337.4 0.5 fusion.42
  338.0 2.4 copy.111
  340.4 14.4 %all-to-all-start.5 = ((bf16[32,128,256]{2,1,0:T(8,128)(2,1)}), bf16[32,128,256]{2,1,0:T(8,128)(2,1)S(1)}, u32[]{:S(2)}, u32[]{:S(2)}) async-start(bf16[32,128,256]{2,1,0:T(8,128)(2,1)} %bitcast.23), calls=%async_computation.5 | async-start | bytes 4194304 | tf_op jit(solution)/shard_map/all_to_all | solution.py:14
  354.8 1.5 reshape.129
  356.3 1.1 convolution_convert_fusion.1
  357.4 26.0 %all-to-all-done.5 = bf16[32,128,256]{2,1,0:T(8,128)(2,1)S(1)} async-done(((bf16[32,128,256]{2,1,0:T(8,128)(2,1)}), bf16[32,128,256]{2,1,0:T(8,128)(2,1)S(1)}, u32[]{:S(2)}, u32[]{:S(2)}) %all-to-all-start.5) | async-done | bytes 2097184 | tf_op jit(solution)/shard_map/all_to_all | solution.py:14
  383.4 0.3 bitcast_reduce_fusion
  384.3 1.0 copy.114
  385.6 1.0 copy.115
  (66 shorter events, 3.8 us)
Async XLA Ops:
  7.2 4.5 %copy-start.17 = (s32[128,1]{0,1:T(1,128)S(1)}, s32[128,1]{0,1:T(1,128)}, u32[]{:S(2)}) copy-start(s32[128,1]{0,1:T(1,128)} %param.10) | copy-start | bytes 1540
  7.2 153.3 %all-gather.10.cloned.1.call-start = ((), (), s32[]{:S(2)}) async-start(), calls=%async_computation.8 | async-start | bytes 4456448 | tf_op jit(solution)/shard_map/all_gather | solution.py:39
  7.9 156.5 %all-gather.8.cloned.1.call-start = ((), (), s32[]{:S(2)}) async-start(), calls=%async_computation.7 | async-start | bytes 4456448 | tf_op jit(solution)/shard_map/all_gather | solution.py:40
  8.7 245.6 %all-gather.6.cloned.1.call-start = ((), (), s32[]{:S(2)}) async-start(), calls=%async_computation.6 | async-start | bytes 4456448 | tf_op jit(solution)/shard_map/all_gather | solution.py:41
  11.8 1.7 copy-start.12
  12.2 11.9 %copy-start.9 = (bf16[128,2048]{1,0:T(8,128)(2,1)S(1)}, bf16[128,2048]{1,0:T(8,128)(2,1)}, u32[]{:S(2)}) copy-start(bf16[128,2048]{1,0:T(8,128)(2,1)} %param.16) | copy-start | bytes 1572868
  13.5 10.9 %copy-start.10 = (bf16[128,2048]{1,0:T(8,128)(2,1)S(1)}, bf16[128,2048]{1,0:T(8,128)(2,1)}, u32[]{:S(2)}) copy-start(bf16[128,2048]{1,0:T(8,128)(2,1)} %param.15) | copy-start | bytes 1572868
  13.5 28.4 %all-to-all-start = ((bf16[32,5,2176]{2,1,0:T(8,128)(2,1)}), bf16[32,5,2176]{2,1,0:T(8,128)(2,1)S(1)}, u32[]{:S(2)}, u32[]{:S(2)}) async-start(bf16[32,5,2176]{2,1,0:T(8,128)(2,1)} %reshape.119), calls=%async_computation | async-start | bytes 2228224 | tf_op jit(solution)/shard_map/all_to_all | solution.py:14
  42.0 2.6 copy-start
  44.5 6.3 %copy-start.1 = (bf16[32,5,2176]{2,1,0:T(8,128)(2,1)S(1)}, bf16[32,5,2176]{2,1,0:T(8,128)(2,1)}, u32[]{:S(2)}) copy-start(bf16[32,5,2176]{2,1,0:T(8,128)(2,1)} %copy-done) | copy-start | bytes 2088964
  44.5 44.9 %all-to-all-start.1 = ((bf16[32,128,384]{1,2,0:T(8,128)(2,1)}), bf16[32,128,384]{1,2,0:T(8,128)(2,1)}, u32[]{:S(2)}, u32[]{:S(2)}) async-start(bf16[32,128,384]{1,2,0:T(8,128)(2,1)} %bitcast.5), calls=%async_computation.1 | async-start | bytes 6291456 | tf_op jit(solution)/shard_map/all_to_all | solution.py:14
  51.3 202.9 %copy-start.14 = (f32[160]{0:T(256)}, f32[160]{0:T(256)S(1)}, u32[]{:S(2)}) copy-start(f32[160]{0:T(256)S(1)} %convert_reduce_fusion) | copy-start | bytes 1924
  92.2 2.3 copy-start.5
  148.6 114.3 %all-to-all-start.2 = ((bf16[32,160,64]{1,2,0:T(8,128)(2,1)}), bf16[32,160,64]{1,2,0:T(8,128)(2,1)}, u32[]{:S(2)}, u32[]{:S(2)}) async-start(bf16[32,160,64]{1,2,0:T(8,128)(2,1)} %copy.96), calls=%async_computation.2 | async-start | bytes 2097152 | tf_op jit(solution)/shard_map/all_to_all | solution.py:14
  262.9 33.7 %all-to-all-start.4 = ((bf16[32,160,64]{1,2,0:T(8,128)(2,1)}), bf16[32,160,64]{1,2,0:T(8,128)(2,1)S(1)}, u32[]{:S(2)}, u32[]{:S(2)}) async-start(bf16[32,160,64]{1,2,0:T(8,128)(2,1)} %copy.98), calls=%async_computation.4 | async-start | bytes 2097152 | tf_op jit(solution)/shard_map/all_to_all | solution.py:14
  279.6 4.2 %copy-start.2 = (bf16[1,2048,1024]{2,1,0:T(8,128)(2,1)S(1)}, bf16[1,2048,1024]{2,1,0:T(8,128)(2,1)}, u32[]{:S(2)}) copy-start(bf16[1,2048,1024]{2,1,0:T(8,128)(2,1)} %all-gather.10.cloned.1.call-done) | copy-start | bytes 12582916
  279.6 4.2 %copy-start.7 = (f32[160,1024]{1,0:T(8,128)S(1)}, f32[160,1024]{1,0:T(8,128)}, u32[]{:S(2)}) copy-start(f32[160,1024]{1,0:T(8,128)} %fusion.4) | copy-start | bytes 1966084
  279.6 4.2 %copy-start.8 = (f32[160,1024]{1,0:T(8,128)S(1)}, f32[160,1024]{1,0:T(8,128)}, u32[]{:S(2)}) copy-start(f32[160,1024]{1,0:T(8,128)} %fusion.8) | copy-start | bytes 1966084
  283.8 2.2 copy-start.3
  283.9 2.2 copy-start.15
  296.6 1.0 copy-start.4
  297.6 42.8 %all-to-all-start.3 = ((bf16[32,5,2048]{2,1,0:T(8,128)(2,1)}), bf16[32,5,2048]{2,1,0:T(8,128)(2,1)}, u32[]{:S(2)}, u32[]{:S(2)}) async-start(bf16[32,5,2048]{2,1,0:T(8,128)(2,1)} %reshape.128), calls=%async_computation.3 | async-start | bytes 2097152 | tf_op jit(solution)/shard_map/all_to_all | solution.py:14
  305.0 1.6 copy-start.11
  311.9 25.3 %copy-start.16 = (pred[16]{0:T(512)(128)(4,1)S(1)}, pred[16]{0:T(512)(128)(4,1)}, u32[]{:S(2)}) copy-start(pred[16]{0:T(512)(128)(4,1)} %iota_compare_fusion.15) | copy-start | bytes 52
  312.5 24.9 %copy-start.6 = (bf16[4096,64]{0,1:T(8,128)(2,1)S(1)}, bf16[4096,64]{0,1:T(8,128)(2,1)}, u32[]{:S(2)}) copy-start(bf16[4096,64]{0,1:T(8,128)(2,1)} %param.17) | copy-start | bytes 1572868
  340.4 15.9 %copy-start.13 = (s32[128]{0:T(128)S(1)}, s32[128]{0:T(128)}, u32[]{:S(2)}) copy-start(s32[128]{0:T(128)} %copy-done.12) | copy-start | bytes 1540
  340.4 43.0 %all-to-all-start.5 = ((bf16[32,128,256]{2,1,0:T(8,128)(2,1)}), bf16[32,128,256]{2,1,0:T(8,128)(2,1)S(1)}, u32[]{:S(2)}, u32[]{:S(2)}) async-start(bf16[32,128,256]{2,1,0:T(8,128)(2,1)} %bitcast.23), calls=%async_computation.5 | async-start | bytes 4194304 | tf_op jit(solution)/shard_map/all_to_all | solution.py:14
Sparse Core Ops, SparseCore 0:
  10.1 74.6 all-gather.9
  86.8 76.3 all-gather.7
  165.2 88.9 all-gather.5
